TPU v7x, 256 devices: a whole 4x4x8 slice. The times are simulated.
256 devices in a mesh: gx: 16 (over z_lo, x, core), gy: 4 (over y), tx: 4 (over z_hi).
Axes of the slice: x: 4, y: 4, z: 8 (z_hi: 4, z_lo: 2; z = z_hi * 2 + z_lo), core: 2. Of those that a mesh axis runs over, the one named last changes fastest.
Arguments:
- src_cell: int32 [8], P('tx'), may hold values from 0 to 524287
- basis: bfloat16 [16, 2, 3, 8, 128, 512], P('tx', None, None, None, 'gx', 'gy'), as said below
- images: bfloat16 [16, 2, 3, 8, 128, 512], P('tx', None, None, None, 'gx', 'gy'), as said below
- induction: bfloat16 [3, 8, 128, 512], P(None, 'tx', 'gx', 'gy'), may hold values from 0.25 to 4
Outputs:
- solution: float32 [8, 2, 3, 8, 128, 512], P('tx', None, None, None, 'gx', 'gy')
- residual: float32 [8, 2, 3, 8, 128, 512], P('tx', None, None, None, 'gx', 'gy')
Inputs may be any that keep to these rules, and one draw needn't show every extreme that they name: `basis`: entries of order one. `images`: entries of order one.
All inputs are finite; a program needn't handle non-finite values.
Results may differ from a plain program's by a relative error of at most 0.0003.
Values may be sent and summed in bfloat16 or wider, within the bound.
No kernel may reach another device: no remote copies, remote signals or barrier semaphores. Data moves between devices by JAX's collectives and lax.ppermute only.
A program may use at most 64 MiB of HBM per device.

v0:
```python
import jax
import jax.numpy as jnp
from jax import lax
from jax.sharding import PartitionSpec as P

CYCLES = 2
ARNOLDI = 2
eps = 1e-06


def with_halo(x, sides, width):
    for axis, dim in sides:
        size, length = (lax.axis_size(axis), x.shape[dim])
        up = [(i, (i + 1) % size) for i in range(size - 1)]
        down = [(j, i) for i, j in up]
        last = lax.slice_in_dim(x, length - width, length, axis=dim)
        initial = lax.slice_in_dim(x, 0, width, axis=dim)
        before = lax.ppermute(last, axis, up)
        after = lax.ppermute(initial, axis, down)
        x = jnp.concatenate([before, x, after], axis=dim)
    return x


def differ(field, axis, forward):
    axis = field.ndim + axis
    count = field.shape[axis]
    delta = lax.slice_in_dim(field, 1, count, axis=axis) - lax.slice_in_dim(
        field, 0, count - 1, axis=axis
    )
    zero = jnp.zeros_like(lax.slice_in_dim(field, 0, 1, axis=axis))
    if forward:
        return jnp.concatenate([delta, zero], axis=axis)
    return jnp.concatenate([zero, delta], axis=axis)


def curl_curl(padded):
    e_x = padded[..., 0, :, :, :]
    e_y = padded[..., 1, :, :, :]
    e_z = padded[..., 2, :, :, :]
    b_x = differ(e_z, -1, True) - differ(e_y, -3, True)
    b_y = differ(e_x, -3, True) - differ(e_z, -2, True)
    b_z = differ(e_y, -2, True) - differ(e_x, -1, True)
    c_x = differ(b_z, -1, False) - differ(b_y, -3, False)
    c_y = differ(b_x, -3, False) - differ(b_z, -2, False)
    c_z = differ(b_y, -2, False) - differ(b_x, -1, False)
    whole = jnp.stack([c_x, c_y, c_z], axis=-4)
    return whole[..., 1:-1, 1:-1, 1:-1]


def apply_operator(field, induct):
    framed = with_halo(field, (("gx", 4), ("gy", 5)), 1)
    padded = jnp.pad(framed, [(0, 0), (0, 0), (0, 0), (1, 1), (0, 0), (0, 0)])
    curled = curl_curl(padded)
    real_part = curled[:, 0] - induct[None] * field[:, 1]
    imag_part = curled[:, 1] + induct[None] * field[:, 0]
    return jnp.stack([real_part, imag_part], axis=1)


def source_field(cells, z_pos, x_pos, y_pos, size_x, size_y, induct):
    plane = size_x * size_y
    src_z = cells // plane
    rest = cells % plane
    src_x = rest // size_y
    src_y = rest % size_y
    d_z = (z_pos[None, :] - src_z[:, None]).astype(jnp.float32)
    d_x = (x_pos[None, :] - src_x[:, None]).astype(jnp.float32)
    d_y = (y_pos[None, :] - src_y[:, None]).astype(jnp.float32)
    dist = jnp.sqrt(
        d_z[:, :, None, None] ** 2 + d_x[:, None, :, None] ** 2 + d_y[:, None, None, :] ** 2
    )
    primary = jnp.exp(-dist / ((size_x + size_y) / 8.0))
    weights = jnp.array([1.0, 0.5, 0.25], dtype=jnp.float32)
    real_part = (induct - 1.0)[None] * weights[None, :, None, None, None] * primary[:, None]
    return jnp.stack([real_part, 0.5 * real_part], axis=1)


def inner_basis(vectors, field):
    return jnp.einsum(
        "kpczxy,spczxy->ks",
        vectors,
        field,
        precision=lax.Precision.HIGHEST,
        preferred_element_type=jnp.float32,
    )


def combine(coeffs, vectors):
    return jnp.einsum(
        "ks,kpczxy->spczxy",
        coeffs,
        vectors,
        precision=lax.Precision.HIGHEST,
        preferred_element_type=jnp.float32,
    )


def per_source(left, right):
    return jnp.sum(left * right, axis=(1, 2, 3, 4, 5))


def expand(values):
    return values[:, None, None, None, None, None]


def small_solve(matrix, rhs):
    factor = jnp.linalg.cholesky(matrix)
    return jax.scipy.linalg.cho_solve((factor, True), rhs)


def on_device(src_cell, basis, images, induction):
    all_basis, all_images, gathered = (
        lax.all_gather(basis, "tx", axis=0, tiled=True),
        lax.all_gather(images, "tx", axis=0, tiled=True),
        lax.all_gather(induction, "tx", axis=1, tiled=True),
    )
    induct = gathered.astype(jnp.float32)
    depth = basis.shape[3]
    width_x = basis.shape[4]
    width_y = basis.shape[5]
    size_x = width_x * lax.axis_size("gx")
    size_y = width_y * lax.axis_size("gy")
    z_pos = jnp.arange(depth, dtype=jnp.int32)
    x_pos = lax.axis_index("gx") * width_x + jnp.arange(width_x, dtype=jnp.int32)
    y_pos = lax.axis_index("gy") * width_y + jnp.arange(width_y, dtype=jnp.int32)
    rhs = source_field(src_cell, z_pos, x_pos, y_pos, size_x, size_y, induct)
    gram_part = jnp.einsum(
        "kpczxy,lpczxy->kl", all_images, all_images, preferred_element_type=jnp.float32
    )
    gram, start_inner = lax.psum((gram_part, inner_basis(all_images, rhs)), ("gx", "gy"))
    factor = jnp.linalg.cholesky(gram)
    h_zero = jax.scipy.linalg.cho_solve((factor, True), start_inner)
    residual = rhs - combine(h_zero, all_images)
    solution = combine(h_zero, all_basis)
    for cycle in range(CYCLES):
        beta = jnp.sqrt(lax.psum(per_source(residual, residual), ("gx", "gy")) + eps)
        krylov = [residual / expand(beta)]
        h_cols = []
        g_cols = []
        for step in range(ARNOLDI):
            work = apply_operator(krylov[step], induct)
            g_raw = lax.psum(inner_basis(all_images, work), ("gx", "gy"))
            g_now = jax.scipy.linalg.cho_solve((factor, True), g_raw)
            work = work - combine(g_now, all_images)
            h_now = lax.psum(jnp.stack([per_source(vec, work) for vec in krylov]), ("gx", "gy"))
            for index in range(step + 1):
                work = work - expand(h_now[index]) * krylov[index]
            h_next = jnp.sqrt(lax.psum(per_source(work, work), ("gx", "gy")) + eps)
            krylov.append(work / expand(h_next))
            pad_rows = jnp.zeros((ARNOLDI - step - 1, h_next.shape[0]), dtype=jnp.float32)
            h_cols.append(jnp.concatenate([h_now, h_next[None], pad_rows], axis=0))
            g_cols.append(g_now)
        hess = jnp.stack(h_cols, axis=1)
        g_all = jnp.stack(g_cols, axis=1)
        normal = jnp.einsum("ijs,iks->sjk", hess, hess, precision=lax.Precision.HIGHEST)
        target = beta[:, None] * jnp.transpose(hess[0])
        y_coef = jax.vmap(small_solve)(normal, target)
        update = expand(y_coef[:, 0]) * krylov[0]
        step = 1
        update = update + expand(y_coef[:, step]) * krylov[step]
        u_coef = jnp.einsum("kjs,sj->ks", g_all, y_coef, precision=lax.Precision.HIGHEST)
        solution = solution + update - combine(u_coef, all_basis)
        first = jnp.zeros((ARNOLDI + 1, beta.shape[0]), dtype=jnp.float32).at[0].set(beta)
        t_coef = first - jnp.einsum("ijs,sj->is", hess, y_coef, precision=lax.Precision.HIGHEST)
        residual = expand(t_coef[0]) * krylov[0]
        for index in range(1, ARNOLDI + 1):
            residual = residual + expand(t_coef[index]) * krylov[index]
    return (solution, residual)


def solution(mesh):
    in_specs = (
        P("tx"),
        P("tx", None, None, None, "gx", "gy"),
        P("tx", None, None, None, "gx", "gy"),
        P(None, "tx", "gx", "gy"),
    )
    out_specs = (P("tx", None, None, None, "gx", "gy"), P("tx", None, None, None, "gx", "gy"))
    return jax.shard_map(
        on_device, mesh=mesh, in_specs=in_specs, out_specs=out_specs, check_vma=False
    )
```

profile of v0, /device:TPU:40, one launch (start us, length us, event | category | flops | bytes accessed | tf_op | source)
XLA Modules:
  0.0 2366.0 jit_solution(5453150176349590648)
XLA Ops:
  7.9 16.6 all_gather.10
  26.5 26.6 %all-gather.3.cloned.1.call-done = bf16[16,2,3,8,8,128]{5,4,3,2,1,0:T(8,128)(2,1)} async-done(((bf16[4,2,3,8,8,128]{5,4,3,2,1,0:T(8,128)(2,1)}), bf16[16,2,3,8,8,128]{5,4,3,2,1,0:T(8,128)(2,1)}) %all-gather.3.cloned.1.call-update) | async-done | bytes 1572880 | tf_op jit(solution)/shard_map/all_gather | solution.py:113
  53.1 5.4 convolution_bitcast_fusion
  58.5 3.7 convolution_bitcast_fusion.8
  62.2 144.3 %all-reduce.54 = (f32[16,2]{0,1:T(2,128)S(1)}, f32[16,16]{0,1:T(8,128)S(1)}) all-reduce(f32[16,2]{0,1:T(2,128)S(1)} %convolution_bitcast_fusion.8, f32[16,16]{0,1:T(8,128)S(1)} %convolution_bitcast_fusion), channel_id=1, replica_groups=mesh['gx'=16,'gy'=4,'tx'=4] {'gx','gy'}, use_global_device_ids=true, to_apply=%region_3.4 | all-reduce | flops 288 | bytes 2304 | tf_op jit(solution)/shard_map/psum | solution.py:129
  214.2 143.8 %psum.114 = f32[2]{0:T(128)S(1)} all-reduce(f32[2]{0:T(128)S(1)} %get-tuple-element.119), channel_id=1, replica_groups=mesh['gx'=16,'gy'=4,'tx'=4] {'gx','gy'}, use_global_device_ids=true, to_apply=%region_5.7 | all-reduce | flops 2 | bytes 16 | tf_op jit(solution)/shard_map/psum | solution.py:135
  360.2 5.8 collective-permute-start.1
  370.4 4.1 collective-permute-start.3
  374.6 4.7 collective-permute-done.2
  394.9 140.9 %psum.115 = f32[16,2]{0,1:T(2,128)S(1)} all-reduce(f32[16,2]{0,1:T(2,128)S(1)} %convolution_bitcast_fusion.7), channel_id=1, replica_groups=mesh['gx'=16,'gy'=4,'tx'=4] {'gx','gy'}, use_global_device_ids=true, to_apply=%region_6.8 | all-reduce | flops 32 | bytes 256 | tf_op jit(solution)/shard_map/psum | solution.py:141
  539.4 139.6 %psum.116 = f32[1,2]{1,0:T(1,128)S(1)} all-reduce(f32[1,2]{1,0:T(1,128)S(1)} %bitcast.337), channel_id=1, replica_groups=mesh['gx'=16,'gy'=4,'tx'=4] {'gx','gy'}, use_global_device_ids=true, to_apply=%region_8.10 | all-reduce | flops 2 | bytes 16 | tf_op jit(solution)/shard_map/psum | solution.py:144
  679.7 139.5 %psum.117 = f32[2]{0:T(128)S(1)} all-reduce(f32[2]{0:T(128)S(1)} %get-tuple-element.49), channel_id=1, replica_groups=mesh['gx'=16,'gy'=4,'tx'=4] {'gx','gy'}, use_global_device_ids=true, to_apply=%region_10.12 | all-reduce | flops 2 | bytes 16 | tf_op jit(solution)/shard_map/psum | solution.py:147
  821.4 5.8 collective-permute-start.5
  831.6 3.9 collective-permute-start.7
  835.6 4.9 collective-permute-done.6
  856.1 141.1 %psum.118 = f32[16,2]{0,1:T(2,128)S(1)} all-reduce(f32[16,2]{0,1:T(2,128)S(1)} %convolution_bitcast_fusion.6), channel_id=1, replica_groups=mesh['gx'=16,'gy'=4,'tx'=4] {'gx','gy'}, use_global_device_ids=true, to_apply=%region_11.13 | all-reduce | flops 32 | bytes 256 | tf_op jit(solution)/shard_map/psum | solution.py:141
  1000.9 139.0 %psum.119 = f32[2,2]{1,0:T(2,128)S(1)} all-reduce(f32[2,2]{1,0:T(2,128)S(1)} %pad_maximum_fusion.26), channel_id=1, replica_groups=mesh['gx'=16,'gy'=4,'tx'=4] {'gx','gy'}, use_global_device_ids=true, to_apply=%region_14.16 | all-reduce | flops 4 | bytes 32 | tf_op jit(solution)/shard_map/psum | solution.py:144
  1140.6 140.2 %psum.120 = f32[2]{0:T(128)S(1)} all-reduce(f32[2]{0:T(128)S(1)} %get-tuple-element.47), channel_id=1, replica_groups=mesh['gx'=16,'gy'=4,'tx'=4] {'gx','gy'}, use_global_device_ids=true, to_apply=%region_16.18 | all-reduce | flops 2 | bytes 16 | tf_op jit(solution)/shard_map/psum | solution.py:147
  1283.8 139.0 %psum.121 = f32[2]{0:T(128)S(1)} all-reduce(f32[2]{0:T(128)S(1)} %get-tuple-element.45), channel_id=1, replica_groups=mesh['gx'=16,'gy'=4,'tx'=4] {'gx','gy'}, use_global_device_ids=true, to_apply=%region_20.24 | all-reduce | flops 2 | bytes 16 | tf_op jit(solution)/shard_map/psum | solution.py:135
  1425.0 5.8 collective-permute-start.9
  1430.8 3.7 convolution_add_fusion
  1437.3 4.1 collective-permute-start.11
  1441.5 5.5 collective-permute-done.10
  1462.7 140.7 %psum.122 = f32[16,2]{0,1:T(2,128)S(1)} all-reduce(f32[16,2]{0,1:T(2,128)S(1)} %convolution_bitcast_fusion.5), channel_id=1, replica_groups=mesh['gx'=16,'gy'=4,'tx'=4] {'gx','gy'}, use_global_device_ids=true, to_apply=%region_21.25 | all-reduce | flops 32 | bytes 256 | tf_op jit(solution)/shard_map/psum | solution.py:141
  1607.0 138.7 %psum.123 = f32[1,2]{1,0:T(1,128)S(1)} all-reduce(f32[1,2]{1,0:T(1,128)S(1)} %bitcast.338), channel_id=1, replica_groups=mesh['gx'=16,'gy'=4,'tx'=4] {'gx','gy'}, use_global_device_ids=true, to_apply=%region_23.27 | all-reduce | flops 2 | bytes 16 | tf_op jit(solution)/shard_map/psum | solution.py:144
  1746.3 140.5 %psum.124 = f32[2]{0:T(128)S(1)} all-reduce(f32[2]{0:T(128)S(1)} %get-tuple-element.43), channel_id=1, replica_groups=mesh['gx'=16,'gy'=4,'tx'=4] {'gx','gy'}, use_global_device_ids=true, to_apply=%region_25.29 | all-reduce | flops 2 | bytes 16 | tf_op jit(solution)/shard_map/psum | solution.py:147
  1889.0 5.8 collective-permute-start.13
  1899.2 3.9 collective-permute-start.15
  1903.2 4.9 collective-permute-done.14
  1923.7 140.9 %psum.125 = f32[16,2]{0,1:T(2,128)S(1)} all-reduce(f32[16,2]{0,1:T(2,128)S(1)} %convolution_bitcast_fusion.4), channel_id=1, replica_groups=mesh['gx'=16,'gy'=4,'tx'=4] {'gx','gy'}, use_global_device_ids=true, to_apply=%region_26.30 | all-reduce | flops 32 | bytes 256 | tf_op jit(solution)/shard_map/psum | solution.py:141
  2068.3 139.0 %psum.126 = f32[2,2]{1,0:T(2,128)S(1)} all-reduce(f32[2,2]{1,0:T(2,128)S(1)} %pad_maximum_fusion.27), channel_id=1, replica_groups=mesh['gx'=16,'gy'=4,'tx'=4] {'gx','gy'}, use_global_device_ids=true, to_apply=%region_29.33 | all-reduce | flops 4 | bytes 32 | tf_op jit(solution)/shard_map/psum | solution.py:144
  2208.7 140.2 %psum.127 = f32[2]{0:T(128)S(1)} all-reduce(f32[2]{0:T(128)S(1)} %get-tuple-element.41), channel_id=1, replica_groups=mesh['gx'=16,'gy'=4,'tx'=4] {'gx','gy'}, use_global_device_ids=true, to_apply=%region_31.35 | all-reduce | flops 2 | bytes 16 | tf_op jit(solution)/shard_map/psum | solution.py:147
  (241 shorter events, 127.9 us)
Async XLA Ops:
  7.2 46.0 %all-gather.3.cloned.1.call-start = ((), (), s32[]{:S(2)}) async-start(), calls=%async_computation | async-start | bytes 1966080 | tf_op jit(solution)/shard_map/all_gather | solution.py:113
  7.9 1422.9 %all-gather.5.cloned.1.call-start = ((), (), s32[]{:S(2)}) async-start(), calls=%async_computation.1 | async-start | bytes 1966080 | tf_op jit(solution)/shard_map/all_gather | solution.py:112
  53.1 5.4 copy-start.1
  358.2 7.7 collective-permute-start
  360.2 7.5 collective-permute-start.1
  368.5 10.8 collective-permute-start.2
  370.4 10.8 collective-permute-start.3
  389.8 1.4 copy-start.2
  819.5 7.8 collective-permute-start.4
  821.4 7.5 collective-permute-start.5
  829.7 10.8 collective-permute-start.6
  831.6 10.8 collective-permute-start.7
  851.0 1.4 copy-start.3
  1423.1 11.5 collective-permute-start.8
  1425.0 9.5 collective-permute-start.9
  1435.4 11.7 collective-permute-start.10
  1437.3 11.7 collective-permute-start.11
  1457.6 1.4 copy-start.4
  1887.0 7.8 collective-permute-start.12
  1889.0 7.5 collective-permute-start.13
  1897.3 10.8 collective-permute-start.14
  1899.2 10.8 collective-permute-start.15
  1918.6 1.4 copy-start.5
  2349.7 4.0 copy-start
Sparse Core Ops, SparseCore 0:
  9.8 43.2 all-gather.2
  366.1 35.2 all-gather.4
where the time goes:
time: 2380 us; the launch traced here: 2370 us
  blocking collectives  2120 us (89%)
  waiting for transfers between devices  59.9 us (3%)
  starting transfers between devices  54.6 us (2%)
  matrix products  50.6 us (2%)
  other arithmetic  50.3 us (2%)
    psum x4, blocking collectives, on_device(): g_raw = lax.psum(inner_basis(all_images, work), ('gx', 'gy'))  564 us
    psum x4, blocking collectives, on_device(): h_next = jnp.sqrt(lax.psum(per_source(work, work), ('gx', 'gy')) + eps)  560 us
    psum x4, blocking collectives, on_device(): lax.psum(jnp.stack([per_source(vec, work) for vec in krylov]), ('gx', 'gy'))  556 us
    psum x2, blocking collectives, on_device(): lax.psum(per_source(residual, residual), ('gx', 'gy')) + eps  283 us
    psum x1, blocking collectives, on_device(): lax.psum((gram_part, inner_basis(all_images, rhs)), ('gx', 'gy'))  144 us
  transfers between devices with their start and end apart: 18, of which 12 were waited for; matrix products, arithmetic and copies ran while one was open for 2% of the time, Pallas kernels for 0%

commit v1 on v0

--- a/solution.py
+++ b/solution.py
@@ -138,7 +138,9 @@
         g_cols = []
         for step in range(ARNOLDI):
             work = apply_operator(krylov[step], induct)
-            g_raw = lax.psum(inner_basis(all_images, work), ("gx", "gy"))
+            own = inner_basis(all_images, work)
+            shards = lax.all_gather(own, ("gx", "gy"))
+            g_raw = jnp.sum(shards, axis=0)
             g_now = jax.scipy.linalg.cho_solve((factor, True), g_raw)
             work = work - combine(g_now, all_images)
             h_now = lax.psum(jnp.stack([per_source(vec, work) for vec in krylov]), ("gx", "gy"))

time: 2380 us -> 2370 us (level)
    psum x4 -> x0, blocking collectives: 564 us -> none  [on_device(): g_raw = lax.psum(inner_basis(all_images, work), ('gx', 'gy'))]
    all_gather x0 -> x4, blocking collectives: none -> 554 us  [on_device(): shards = lax.all_gather(own, ('gx', 'gy'))]
where the time goes in v1:
time: 2370 us; the launch traced here: 2360 us
  blocking collectives  2110 us (89%)
  waiting for transfers between devices  59.9 us (3%)
  starting transfers between devices  54.6 us (2%)
  other arithmetic  50.6 us (2%)
  matrix products  50.6 us (2%)
    psum x4, blocking collectives, on_device(): h_next = jnp.sqrt(lax.psum(per_source(work, work), ('gx', 'gy')) + eps)  561 us
    psum x4, blocking collectives, on_device(): lax.psum(jnp.stack([per_source(vec, work) for vec in krylov]), ('gx', 'gy'))  556 us
    all_gather x4, blocking collectives, on_device(): shards = lax.all_gather(own, ('gx', 'gy'))  554 us
    psum x2, blocking collectives, on_device(): lax.psum(per_source(residual, residual), ('gx', 'gy')) + eps  283 us
    psum x1, blocking collectives, on_device(): lax.psum((gram_part, inner_basis(all_images, rhs)), ('gx', 'gy'))  144 us
  transfers between devices with their start and end apart: 18, of which 12 were waited for; matrix products, arithmetic and copies ran while one was open for 2% of the time, Pallas kernels for 0%

profile of v1, /device:TPU:40, one launch (start us, length us, event | category | flops | bytes accessed | tf_op | source)
XLA Modules:
  0.0 2356.7 jit_solution(5946858598461464505)
XLA Ops:
  7.9 16.6 all_gather.34
  26.5 26.6 %all-gather.11.cloned.1.call-done = bf16[16,2,3,8,8,128]{5,4,3,2,1,0:T(8,128)(2,1)} async-done(((bf16[4,2,3,8,8,128]{5,4,3,2,1,0:T(8,128)(2,1)}), bf16[16,2,3,8,8,128]{5,4,3,2,1,0:T(8,128)(2,1)}) %all-gather.11.cloned.1.call-update) | async-done | bytes 1572880 | tf_op jit(solution)/shard_map/all_gather | solution.py:113
  53.1 5.4 convolution_bitcast_fusion
  58.5 3.7 convolution_bitcast_fusion.8
  62.2 144.3 %all-reduce.54 = (f32[16,2]{0,1:T(2,128)S(1)}, f32[16,16]{0,1:T(8,128)S(1)}) all-reduce(f32[16,2]{0,1:T(2,128)S(1)} %convolution_bitcast_fusion.8, f32[16,16]{0,1:T(8,128)S(1)} %convolution_bitcast_fusion), channel_id=1, replica_groups=mesh['gx'=16,'gy'=4,'tx'=4] {'gx','gy'}, use_global_device_ids=true, to_apply=%region_3.4 | all-reduce | flops 288 | bytes 2304 | tf_op jit(solution)/shard_map/psum | solution.py:129
  214.2 143.8 %psum.86 = f32[2]{0:T(128)S(1)} all-reduce(f32[2]{0:T(128)S(1)} %get-tuple-element.119), channel_id=1, replica_groups=mesh['gx'=16,'gy'=4,'tx'=4] {'gx','gy'}, use_global_device_ids=true, to_apply=%region_5.7 | all-reduce | flops 2 | bytes 16 | tf_op jit(solution)/shard_map/psum | solution.py:135
  360.2 5.8 collective-permute-start.1
  370.4 4.1 collective-permute-start.3
  374.6 4.7 collective-permute-done.2
  394.9 138.5 %all-gather.4 = f32[64,16,2]{1,2,0:T(2,128)S(1)} all-gather(f32[1,16,2]{1,2,0:T(2,128)S(1)} %convolution_bitcast_fusion.7), channel_id=2, replica_groups=mesh['gx'=16,'gy'=4,'tx'=4] {'gx','gy'}, dimensions={0}, use_global_device_ids=true | all-gather | bytes 8320 | tf_op jit(solution)/shard_map/all_gather | solution.py:142
  537.0 139.0 %psum.87 = f32[1,2]{1,0:T(1,128)S(1)} all-reduce(f32[1,2]{1,0:T(1,128)S(1)} %bitcast.345), channel_id=1, replica_groups=mesh['gx'=16,'gy'=4,'tx'=4] {'gx','gy'}, use_global_device_ids=true, to_apply=%region_8.10 | all-reduce | flops 2 | bytes 16 | tf_op jit(solution)/shard_map/psum | solution.py:146
  676.7 140.2 %psum.88 = f32[2]{0:T(128)S(1)} all-reduce(f32[2]{0:T(128)S(1)} %get-tuple-element.49), channel_id=1, replica_groups=mesh['gx'=16,'gy'=4,'tx'=4] {'gx','gy'}, use_global_device_ids=true, to_apply=%region_10.12 | all-reduce | flops 2 | bytes 16 | tf_op jit(solution)/shard_map/psum | solution.py:149
  819.0 5.8 collective-permute-start.5
  829.3 3.9 collective-permute-start.7
  833.3 4.9 collective-permute-done.6
  853.7 138.7 %all-gather.5 = f32[64,16,2]{1,2,0:T(2,128)S(1)} all-gather(f32[1,16,2]{1,2,0:T(2,128)S(1)} %convolution_bitcast_fusion.6), channel_id=3, replica_groups=mesh['gx'=16,'gy'=4,'tx'=4] {'gx','gy'}, dimensions={0}, use_global_device_ids=true | all-gather | bytes 8320 | tf_op jit(solution)/shard_map/all_gather | solution.py:142
  996.2 139.0 %psum.89 = f32[2,2]{1,0:T(2,128)S(1)} all-reduce(f32[2,2]{1,0:T(2,128)S(1)} %pad_maximum_fusion.26), channel_id=1, replica_groups=mesh['gx'=16,'gy'=4,'tx'=4] {'gx','gy'}, use_global_device_ids=true, to_apply=%region_14.16 | all-reduce | flops 4 | bytes 32 | tf_op jit(solution)/shard_map/psum | solution.py:146
  1136.0 140.2 %psum.90 = f32[2]{0:T(128)S(1)} all-reduce(f32[2]{0:T(128)S(1)} %get-tuple-element.47), channel_id=1, replica_groups=mesh['gx'=16,'gy'=4,'tx'=4] {'gx','gy'}, use_global_device_ids=true, to_apply=%region_16.18 | all-reduce | flops 2 | bytes 16 | tf_op jit(solution)/shard_map/psum | solution.py:149
  1279.1 139.0 %psum.91 = f32[2]{0:T(128)S(1)} all-reduce(f32[2]{0:T(128)S(1)} %get-tuple-element.45), channel_id=1, replica_groups=mesh['gx'=16,'gy'=4,'tx'=4] {'gx','gy'}, use_global_device_ids=true, to_apply=%region_20.24 | all-reduce | flops 2 | bytes 16 | tf_op jit(solution)/shard_map/psum | solution.py:135
  1420.4 5.8 collective-permute-start.9
  1426.2 3.7 convolution_add_fusion
  1432.7 4.1 collective-permute-start.11
  1436.9 5.5 collective-permute-done.10
  1458.0 138.3 %all-gather.6 = f32[64,16,2]{1,2,0:T(2,128)S(1)} all-gather(f32[1,16,2]{1,2,0:T(2,128)S(1)} %convolution_bitcast_fusion.5), channel_id=4, replica_groups=mesh['gx'=16,'gy'=4,'tx'=4] {'gx','gy'}, dimensions={0}, use_global_device_ids=true | all-gather | bytes 8320 | tf_op jit(solution)/shard_map/all_gather | solution.py:142
  1600.0 138.7 %psum.92 = f32[1,2]{1,0:T(1,128)S(1)} all-reduce(f32[1,2]{1,0:T(1,128)S(1)} %bitcast.346), channel_id=1, replica_groups=mesh['gx'=16,'gy'=4,'tx'=4] {'gx','gy'}, use_global_device_ids=true, to_apply=%region_23.27 | all-reduce | flops 2 | bytes 16 | tf_op jit(solution)/shard_map/psum | solution.py:146
  1739.3 140.5 %psum.93 = f32[2]{0:T(128)S(1)} all-reduce(f32[2]{0:T(128)S(1)} %get-tuple-element.43), channel_id=1, replica_groups=mesh['gx'=16,'gy'=4,'tx'=4] {'gx','gy'}, use_global_device_ids=true, to_apply=%region_25.29 | all-reduce | flops 2 | bytes 16 | tf_op jit(solution)/shard_map/psum | solution.py:149
  1882.0 5.8 collective-permute-start.13
  1892.2 3.9 collective-permute-start.15
  1896.2 4.9 collective-permute-done.14
  1916.7 138.5 %all-gather.7 = f32[64,16,2]{1,2,0:T(2,128)S(1)} all-gather(f32[1,16,2]{1,2,0:T(2,128)S(1)} %convolution_bitcast_fusion.4), channel_id=5, replica_groups=mesh['gx'=16,'gy'=4,'tx'=4] {'gx','gy'}, dimensions={0}, use_global_device_ids=true | all-gather | bytes 8320 | tf_op jit(solution)/shard_map/all_gather | solution.py:142
  2059.0 139.0 %psum.94 = f32[2,2]{1,0:T(2,128)S(1)} all-reduce(f32[2,2]{1,0:T(2,128)S(1)} %pad_maximum_fusion.27), channel_id=1, replica_groups=mesh['gx'=16,'gy'=4,'tx'=4] {'gx','gy'}, use_global_device_ids=true, to_apply=%region_29.33 | all-reduce | flops 4 | bytes 32 | tf_op jit(solution)/shard_map/psum | solution.py:146
  2199.4 140.2 %psum.95 = f32[2]{0:T(128)S(1)} all-reduce(f32[2]{0:T(128)S(1)} %get-tuple-element.41), channel_id=1, replica_groups=mesh['gx'=16,'gy'=4,'tx'=4] {'gx','gy'}, use_global_device_ids=true, to_apply=%region_31.35 | all-reduce | flops 2 | bytes 16 | tf_op jit(solution)/shard_map/psum | solution.py:149
  (245 shorter events, 128.3 us)
Async XLA Ops:
  7.2 46.0 %all-gather.11.cloned.1.call-start = ((), (), s32[]{:S(2)}) async-start(), calls=%async_computation | async-start | bytes 1966080 | tf_op jit(solution)/shard_map/all_gather | solution.py:113
  7.9 1418.3 %all-gather.13.cloned.1.call-start = ((), (), s32[]{:S(2)}) async-start(), calls=%async_computation.1 | async-start | bytes 1966080 | tf_op jit(solution)/shard_map/all_gather | solution.py:112
  53.1 5.4 copy-start.1
  358.2 7.7 collective-permute-start
  360.2 7.5 collective-permute-start.1
  368.5 10.8 collective-permute-start.2
  370.4 10.8 collective-permute-start.3
  389.8 1.4 copy-start.2
  817.1 7.8 collective-permute-start.4
  819.0 7.5 collective-permute-start.5
  827.3 10.8 collective-permute-start.6
  829.3 10.8 collective-permute-start.7
  848.7 1.4 copy-start.3
  1418.4 11.5 collective-permute-start.8
  1420.4 9.5 collective-permute-start.9
  1430.7 11.7 collective-permute-start.10
  1432.7 11.7 collective-permute-start.11
  1452.9 1.4 copy-start.4
  1880.0 7.8 collective-permute-start.12
  1882.0 7.5 collective-permute-start.13
  1890.3 10.8 collective-permute-start.14
  1892.2 10.8 collective-permute-start.15
  1911.6 1.4 copy-start.5
  2340.4 4.0 copy-start
Sparse Core Ops, SparseCore 0:
  9.8 43.2 all-gather.10
  366.1 35.2 all-gather.12
